TPU v7x, 256 devices: a whole 4x4x8 slice. The times are simulated.
256 devices in a mesh: seq: 64 (over x_hi, y, z), head: 4 (over x_lo, core).
Axes of the slice: x: 4 (x_hi: 2, x_lo: 2; x = x_hi * 2 + x_lo), y: 4, z: 8, core: 2. Of those that a mesh axis runs over, the one named last changes fastest.
Arguments:
- queries: bfloat16 [98304, 2048], P('seq', 'head'), may hold values from -200 to 200
- keys_values: bfloat16 [2, 98304, 2048], P(None, 'seq', 'head'), may hold values from -6 to 6
- global_ids: int32 [2], replicated, may hold values from 0 to 1535
- rand_ids: int32 [1536, 3], replicated, may hold values from 0 to 1535, as said below
- out_weight: bfloat16 [2048, 4096], P(None, 'head'), may hold values from -2 to 2
Outputs:
- projected: bfloat16 [98304, 4096], P('seq', 'head')
Inputs may be any that keep to these rules, and one draw needn't show every extreme that they name: `rand_ids`: row i lists the 3 random key blocks of query block i. Among the 24 rows of one seq shard, at most 2 listed blocks lie on any one shard, and at most 1 of one column do; both bounds are reached.
All inputs are finite; a program needn't handle non-finite values.
Results may differ from a plain program's by a relative error of at most 0.0057.
Values may be sent and summed in bfloat16 or wider, within the bound.
A program may use at most 128 MiB of HBM per device.

v0:
```python
import jax
import jax.numpy as jnp
from jax import lax
from jax.sharding import PartitionSpec as P

HEAD_DIM = 128
BLOCK = 64
NGLOBAL = 2
NRANDOM = 3


group_blocks = 8


def padded_2(block, sides, width):
    for axis, dim in sides:
        count = lax.axis_size(axis)
        forward = [(i, i + 1) for i in range(count - 1)]
        backward = [(target, source) for source, target in forward]
        low = lax.ppermute(
            lax.slice_in_dim(block, block.shape[dim] - width, None, axis=dim), axis, forward
        )
        high = lax.ppermute(lax.slice_in_dim(block, 0, width, axis=dim), axis, backward)
        block = jnp.concatenate([low, block, high], axis=dim)
    return block


def broadcast(block, axis, owner):
    block = jnp.where(lax.axis_index(axis) == owner, block, jnp.zeros_like(block))
    return lax.psum(block, axis)


def plan_slots(requests, myself, capacity, per_shard):
    sources = requests // per_shard
    offsets = requests % per_shard
    count = requests.shape[1]
    order = jnp.arange(count, dtype=jnp.int32)
    earlier = (order[:, None] < order[None, :]).astype(jnp.int32)
    matches = (sources[:, :, None] == sources[:, None, :]).astype(jnp.int32)
    ranks = jnp.sum(matches * earlier[None], axis=1)
    slot_range = jnp.arange(capacity, dtype=jnp.int32)
    wanted = (
        (sources == myself)[:, None, :] & (ranks[:, None, :] == slot_range[None, :, None])
    ).astype(jnp.int32)
    chosen = jnp.sum(wanted * offsets[:, None, :], axis=2).reshape(-1)
    own_sources = lax.dynamic_index_in_dim(sources, myself, 0, keepdims=False)
    own_ranks = lax.dynamic_index_in_dim(ranks, myself, 0, keepdims=False)
    return (chosen, own_sources * capacity + own_ranks)


def attend_blocks(query_part, local_keys, local_values, glob_keys, glob_values, valid):
    scale = 1.0 / HEAD_DIM**0.5
    near_scores = (
        jnp.einsum("bqhd,bkhd->bhqk", query_part, local_keys, preferred_element_type=jnp.float32)
        * scale
    )
    near_scores = jnp.where(valid[:, None, None, :], near_scores, -jnp.inf)
    glob_scores = (
        jnp.einsum("bqhd,khd->bhqk", query_part, glob_keys, preferred_element_type=jnp.float32)
        * scale
    )
    highest = jnp.maximum(jnp.max(near_scores, axis=-1), jnp.max(glob_scores, axis=-1))
    near_exp = jnp.exp(near_scores - highest[..., None])
    glob_exp = jnp.exp(glob_scores - highest[..., None])
    total = jnp.sum(near_exp, axis=-1) + jnp.sum(glob_exp, axis=-1)
    near_weights = (near_exp / total[..., None]).astype(jnp.bfloat16)
    glob_weights = (glob_exp / total[..., None]).astype(jnp.bfloat16)
    mixed = jnp.einsum(
        "bhqk,bkhd->bqhd", near_weights, local_values, preferred_element_type=jnp.float32
    )
    mixed = mixed + jnp.einsum(
        "bhqk,khd->bqhd", glob_weights, glob_values, preferred_element_type=jnp.float32
    )
    return mixed.astype(jnp.bfloat16)


def body(queries, keys_values, global_ids, rand_ids, out_weight):
    rows = queries.shape[0]
    width = queries.shape[1]
    heads_here = width // HEAD_DIM
    local_blocks = rows // BLOCK
    shards = lax.axis_size("seq")
    myself = lax.axis_index("seq")
    total_blocks = local_blocks * shards
    pair_blocks = keys_values.reshape(2, local_blocks, BLOCK, width)
    padded = padded_2(keys_values, (("seq", 1),), BLOCK)
    padded = padded.reshape(2, local_blocks + 2, BLOCK, width)
    panel_list = []
    for which in range(NGLOBAL):
        target = global_ids[which]
        owner = target // local_blocks
        local_panel = lax.dynamic_index_in_dim(
            pair_blocks, target % local_blocks, 1, keepdims=False
        )
        panel_list.append(broadcast(local_panel, "seq", owner))
    glob = jnp.stack(panel_list, axis=1).reshape(2, NGLOBAL * BLOCK, heads_here, HEAD_DIM)
    requests = rand_ids.reshape(shards, local_blocks, NRANDOM)
    capacity = (local_blocks + shards - 1) // shards
    fetched = []
    for column in range(NRANDOM):
        chosen, slots = plan_slots(requests[:, :, column], myself, capacity, local_blocks)
        outgoing = jnp.take(pair_blocks, chosen, axis=1)
        incoming = lax.all_to_all(outgoing, "seq", split_axis=1, concat_axis=1, tiled=True)
        fetched.append(jnp.take(incoming, slots, axis=1))
    remote = jnp.stack(fetched, axis=2)
    segment = jnp.arange((3 + NRANDOM) * BLOCK, dtype=jnp.int32) // BLOCK

    def one_group(index):
        first = index * group_blocks
        query_part = lax.dynamic_slice_in_dim(queries, first * BLOCK, group_blocks * BLOCK, 0)
        query_part = query_part.reshape(group_blocks, BLOCK, heads_here, HEAD_DIM)
        window = lax.dynamic_slice_in_dim(padded, first, group_blocks + 2, 1)
        farther = lax.dynamic_slice_in_dim(remote, first, group_blocks, 1)
        farther = farther.reshape(2, group_blocks, NRANDOM * BLOCK, width)
        local = jnp.concatenate(
            [
                window[:, 0:group_blocks],
                window[:, 1 : group_blocks + 1],
                window[:, 2 : group_blocks + 2],
                farther,
            ],
            axis=2,
        )
        local = local.reshape(2, group_blocks, (3 + NRANDOM) * BLOCK, heads_here, HEAD_DIM)
        block_ids = myself * local_blocks + first + jnp.arange(group_blocks, dtype=jnp.int32)
        drop_before = (segment[None, :] == 0) & (block_ids[:, None] == 0)
        drop_after = (segment[None, :] == 2) & (block_ids[:, None] == total_blocks - 1)
        valid = jnp.logical_not(drop_before | drop_after)
        mixed = attend_blocks(query_part, local[0], local[1], glob[0], glob[1], valid)
        return mixed.reshape(group_blocks * BLOCK, width)

    attended = lax.map(
        one_group, jnp.arange(local_blocks // group_blocks, dtype=jnp.int32)
    ).reshape(rows, width)
    summed = jnp.dot(
        lax.all_gather(attended, "head", axis=1, tiled=True),
        out_weight,
        preferred_element_type=jnp.float32,
    )
    return summed.astype(jnp.bfloat16)


def solution(mesh):
    in_specs = (P("seq", "head"), P(None, "seq", "head"), P(), P(), P(None, "head"))
    out_specs = P("seq", "head")
    return jax.shard_map(body, mesh=mesh, in_specs=in_specs, out_specs=out_specs, check_vma=False)
```

profile of v0, /device:TPU:97, one launch (start us, length us, event | category | flops | bytes accessed | tf_op | source)
XLA Modules:
  0.0 1350.5 jit_solution(5042256346633394672)
XLA Ops:
  8.1 7.1 gather_fusion.2
  15.2 7.5 select_bitcast_fusion.1
  22.7 13.3 all-to-all-start.1
  36.1 5.5 gather_fusion
  41.7 7.5 select_bitcast_fusion.2
  49.1 170.3 %all-to-all-done.1 = bf16[2,64,64,512]{3,2,0,1:T(8,128)(2,1)} async-done(((bf16[2,64,64,512]{3,2,0,1:T(8,128)(2,1)}), bf16[2,64,64,512]{3,2,0,1:T(8,128)(2,1)}, u32[]{:S(2)}, u32[]{:S(2)}) %all-to-all-start.1) | async-done | bytes 8388640 | tf_op jit(solution)/shard_map/all_to_all | solution.py:103
  219.4 12.3 all-to-all-start
  231.7 5.5 gather_fusion.4
  237.2 7.5 select_bitcast_fusion
  244.7 170.2 %all-to-all-done = bf16[2,64,64,512]{3,2,0,1:T(8,128)(2,1)} async-done(((bf16[2,64,64,512]{3,2,0,1:T(8,128)(2,1)}), bf16[2,64,64,512]{3,2,0,1:T(8,128)(2,1)}, u32[]{:S(2)}, u32[]{:S(2)}) %all-to-all-start) | async-done | bytes 8388640 | tf_op jit(solution)/shard_map/all_to_all | solution.py:103
  414.9 12.5 all-to-all-start.2
  444.1 170.6 %collective-permute-done = bf16[2,64,512]{2,1,0:T(8,128)(2,1)S(1)} collective-permute-done((bf16[2,64,512]{2,1,0:T(8,128)(2,1)S(1)}, bf16[2,64,512]{2,1,0:T(8,128)(2,1)S(1)}, u32[]{:S(2)}, u32[]{:S(2)}) %collective-permute-start) | collective-permute-done | bytes 131104 | tf_op jit(solution)/shard_map/ppermute | solution.py:20
  617.4 446.9 %all-reduce.3.cloned.1.call-done = (bf16[2,1,64,512]{3,2,1,0:T(8,128)(2,1)}, bf16[2,1,64,512]{3,2,1,0:T(8,128)(2,1)}) async-done(((bf16[2,1,64,512]{3,2,1,0:T(8,128)(2,1)}, bf16[2,1,64,512]{3,2,1,0:T(8,128)(2,1)}), (bf16[2,1,64,512]{3,2,1,0:T(8,128)(2,1)}, bf16[2,1,64,512]{3,2,1,0:T(8,128)(2,1)})) %all-reduce.3.cloned.1.call-update) | async-done | bytes 262160 | tf_op jit(solution)/shard_map/psum | solution.py:30
  1065.4 7.7 copy.122
  1073.1 5.9 gather_fusion.3
  1079.0 7.7 copy.120
  1086.7 5.9 gather_fusion.1
  1097.5 7.7 copy.124
  1105.2 5.9 gather_fusion.5
  1118.1 114.5 %while.14 = (s32[]{:T(128)}, bf16[3,512,512]{2,1,0:T(8,128)(2,1)}, s32[3]{0:T(128)S(1)}, bf16[2,26,64,512]{3,2,1,0:T(8,128)(2,1)}, bf16[2,24,3,64,512]{4,3,0,1,2...) while((s32[]{:T(128)}, bf16[3,512,512]{2,1,0:T(8,128)(2,1)}, ...), condition=%wide.region_13.16_spmd.clone.clone, body=%wide.region_8.15_spmd.clone.clone.sunk | while | flops 573845248 | bytes 120519192 | solution.py:132
  1124.2 4.8 pad_maximum_fusion.5
  1162.5 4.8 pad_maximum_fusion.5
  1232.7 99.9 %all-gather.2.cloned.1.call-done = bf16[1536,2048]{1,0:T(8,128)(2,1)} async-done(((bf16[1536,512]{1,0:T(8,128)(2,1)}), bf16[1536,2048]{1,0:T(8,128)(2,1)}) %all-gather.2.cloned.1.call-update) | async-done | bytes 6291472 | tf_op jit(solution)/shard_map/all_gather | solution.py:136
  1332.5 11.1 convolution_convert_fusion
  (183 shorter events, 131.1 us)
Async XLA Ops:
  7.6 7.6 copy-start.8
  7.7 7.5 copy-start.9
  8.0 7.3 copy-start.11
  8.0 7.3 copy-start.12
  8.0 28.1 %copy-start.10 = (s32[64,24]{0,1:T(8,128)}, s32[64,24]{0,1:T(8,128)S(1)}, u32[]{:S(2)}) copy-start(s32[64,24]{0,1:T(8,128)S(1)} %get-tuple-element.222) | copy-start | bytes 18436
  22.7 13.4 copy-start.2
  22.7 196.7 %all-to-all-start.1 = ((bf16[2,64,64,512]{3,2,0,1:T(8,128)(2,1)}), bf16[2,64,64,512]{3,2,0,1:T(8,128)(2,1)}, u32[]{:S(2)}, u32[]{:S(2)}) async-start(bf16[2,64,64,512]{3,2,0,1:T(8,128)(2,1)} %select_bitcast_fusion.1), calls=%async_computation.1 | async-start | bytes 16777216 | tf_op jit(solution)/shard_map/all_to_all | solution.py:103
  219.4 195.5 %all-to-all-start = ((bf16[2,64,64,512]{3,2,0,1:T(8,128)(2,1)}), bf16[2,64,64,512]{3,2,0,1:T(8,128)(2,1)}, u32[]{:S(2)}, u32[]{:S(2)}) async-start(bf16[2,64,64,512]{3,2,0,1:T(8,128)(2,1)} %select_bitcast_fusion.2), calls=%async_computation | async-start | bytes 16777216 | tf_op jit(solution)/shard_map/all_to_all | solution.py:103
  244.7 189.0 %copy-start.14 = (s32[2]{0:T(128)S(1)}, s32[2]{0:T(128)}, u32[]{:S(2)}) copy-start(s32[2]{0:T(128)} %param.13) | copy-start | bytes 28
  414.9 682.6 %all-to-all-start.2 = ((bf16[2,64,64,512]{3,2,0,1:T(8,128)(2,1)}), bf16[2,64,64,512]{3,2,0,1:T(8,128)(2,1)}, u32[]{:S(2)}, u32[]{:S(2)}) async-start(bf16[2,64,64,512]{3,2,0,1:T(8,128)(2,1)} %select_bitcast_fusion), calls=%async_computation.2 | async-start | bytes 16777216 | tf_op jit(solution)/shard_map/all_to_all | solution.py:103
  427.4 636.9 %all-reduce.3.cloned.1.call-start = ((), (), s32[]{:S(2)}) async-start(), calls=%async_computation.4 | async-start | bytes 524288 | tf_op jit(solution)/shard_map/psum | solution.py:30
  427.5 187.2 %collective-permute-start = (bf16[2,64,512]{2,1,0:T(8,128)(2,1)S(1)}, bf16[2,64,512]{2,1,0:T(8,128)(2,1)S(1)}, u32[]{:S(2)}, u32[]{:S(2)}) collective-permute-start(bf16[2,64,512]{2,1,0:T(8,128)(2,1)S(1)} %get-tuple-element.258), channel_id=1, source_target_pairs={{0,4},{4,8},{8,12},{12,16},{16,20},{20,24},{24,28},{28,32},{32,36}... | collective-permute-start | bytes 393224 | tf_op jit(solution)/shard_map/ppermute | solution.py:20
  431.8 182.9 %collective-permute-start.1 = (bf16[2,64,512]{2,1,0:T(8,128)(2,1)S(1)}, bf16[2,64,512]{2,1,0:T(8,128)(2,1)}, u32[]{:S(2)}, u32[]{:S(2)}) collective-permute-start(bf16[2,64,512]{2,1,0:T(8,128)(2,1)S(1)} %get-tuple-element.259), channel_id=1, source_target_pairs={{4,0},{8,4},{12,8},{16,12},{20,16},{24,20},{28,24},{32,28},{36,32}... | collective-permute-start | bytes 393224 | tf_op jit(solution)/shard_map/ppermute | solution.py:23
  438.7 893.8 %all-gather.2.cloned.1.call-start = ((), (), s32[]{:S(2)}) async-start(), calls=%async_computation.3 | async-start | bytes 7864320 | tf_op jit(solution)/shard_map/all_gather | solution.py:136
  1086.7 5.9 copy-start.13
  1142.8 3.0 copy-start.4
  1145.8 4.8 copy-start.1
  1150.6 3.4 copy-start.5
  1181.0 3.0 copy-start.4
  1184.0 4.8 copy-start.1
  1188.8 3.4 copy-start.5
  1219.1 3.0 copy-start.4
  1222.1 4.8 copy-start.1
  1226.9 3.4 copy-start.5
  (9 other events, 19.3 us)
Sparse Core Ops, SparseCore 0:
  438.8 625.4 all-reduce.2
  1232.8 99.6 all-gather.1
where the time goes:
time: 1350 us
  waiting for transfers between devices  1060 us (79%)
  local copies, waits for them, and re-layouts  132 us (10%)
  other arithmetic  63.6 us (5%)
  starting transfers between devices  44.5 us (3%)
  matrix products  31.4 us (2%)
  between operations  17.4 us (1%)
    psum x1, waiting for transfers between devices, broadcast(): return lax.psum(block, axis)  447 us
    all_to_all x3, waiting for transfers between devices, body(): lax.all_to_all(outgoing, 'seq', split_axis=1, concat_axis=1, tiled=True)  341 us
    ppermute x1, waiting for transfers between devices, padded_2(): lax.ppermute(lax.slice_in_dim(block, block.shape[dim] - width, None, axis...  171 us
    all_gather x1, waiting for transfers between devices, body(): lax.all_gather(attended, 'head', axis=1, tiled=True)  99.9 us
    all_to_all x3, starting transfers between devices, body(): lax.all_to_all(outgoing, 'seq', split_axis=1, concat_axis=1, tiled=True)  38.1 us
  transfers between devices with their start and end apart: 7, of which 5 were waited for; matrix products, arithmetic and copies ran while one was open for 5% of the time, Pallas kernels for 0%

commit v1 on v0

v1 whole, which is shorter than its diff:
```python
import functools
import math

import jax
import jax.numpy as jnp
from jax import lax
from jax.experimental import pallas as pl
from jax.experimental.pallas import tpu as pltpu
from jax.sharding import PartitionSpec as P

HEAD_DIM = 128
BLOCK = 64
NGLOBAL = 2
NRANDOM = 3
MESH = pl.DeviceIdType.MESH

NXH, NY, NZ, NXL, NC = 2, 4, 8, 2, 2
LINES = NXH * NY
SHARD_BLOCKS = 24
ROWS = SHARD_BLOCKS * BLOCK
HALF_BLOCKS = SHARD_BLOCKS // NC
HALF = HALF_BLOCKS * BLOCK
LINE_BLOCKS = NZ * SHARD_BLOCKS
Q_BLOCKS = NZ * HALF_BLOCKS


def coords():
    seq = lax.axis_index("seq")
    head = lax.axis_index("head")
    return seq // (NY * NZ), (seq // NZ) % NY, seq % NZ, head // NC, head % NC


def device(xh, y, z, xl, c):
    return ((xh * NY + y) * NZ + z, xl * NC + c)


def remote(src, dst, send_sem, recv_sem, target):
    return pltpu.make_async_remote_copy(
        src_ref=src, dst_ref=dst, send_sem=send_sem, recv_sem=recv_sem,
        device_id=target, device_id_type=MESH,
    )


def nearest(k):
    return (k % 2) * ((k + 1) // 2) - (1 - k % 2) * (k // 2)


(KX, VX0, VX1, VX2, VX3, KU, KD, VU, VD, K2U, K2D, KFU, KFD, VFU, VFD, KF2U, KF2D) = range(17)
NCLASS = 17


def gather_kernel(q_ref, kv_ref, full_ref, qr_ref, zs, zr, ss, rs, bs, br):
    xh, y, z, xl, c = coords()
    line = xh * NY + y
    up, down, opp = (y + 1) % NY, (y + NY - 1) % NY, (y + 2) % NY
    ox = 1 - xh
    to_x, to_up, to_down = device(ox, y, z, xl, c), device(xh, up, z, xl, c), device(xh, down, z, xl, c)
    to_sib = device(xh, y, z, xl, 1 - c)

    barrier = pltpu.get_barrier_semaphore()
    friends = [
        device(xh, y, (z + dz) % NZ, xl, (c + dc) % NC)
        for dz in range(NZ) for dc in range(NC) if dz or dc
    ] + [to_x, to_up, to_down]
    for friend in friends:
        pl.semaphore_signal(barrier, inc=1, device_id=friend, device_id_type=MESH)
    pl.semaphore_wait(barrier, len(friends))

    def z_parts(t, kind, half):
        cols = pl.ds(pl.multiple_of((t - 4 * c) * HEAD_DIM, HEAD_DIM), HEAD_DIM)
        rows = pl.ds(half * HALF, HALF)
        if kind == 2:
            return q_ref.at[rows, cols], qr_ref.at[z]
        return kv_ref.at[kind, rows, cols], full_ref.at[kind, line, half, z]

    def z_each(k, kinds, remote_fn, local_fn):
        t = (z + nearest(k) + NZ) % NZ

        @pl.when(t // 4 == c)
        def _():
            for kind in kinds:
                for half in range(NC):
                    src, dst = z_parts(t, kind, half)
                    mine = jnp.logical_and(t == z, c == half)
                    if local_fn is not None:
                        @pl.when(mine)
                        def _():
                            local_fn(pltpu.make_async_copy(src, dst, zr.at[kind, z]))

                    @pl.when(jnp.logical_not(mine))
                    def _():
                        remote_fn(remote(src, dst, zs.at[kind, half, k], zr.at[kind, z],
                                         device(xh, y, t, xl, half)))

    @pl.loop(0, NZ)
    def _(k):
        z_each(k, (0, 1), lambda d: d.start(), lambda d: d.start())

    @pl.loop(0, NZ)
    def _(k):
        z_each(k, (2,), lambda d: d.start(), lambda d: d.start())

    H = HALF // 2

    def part(kv, ln, p, rows=None):
        ref = full_ref.at[kv, ln, c, p]
        return ref if rows is None else ref.at[pl.ds(rows * H, H)]

    def copy(cls, k, p, kv, ln, target, rows=None):
        ref = part(kv, ln, p, rows)
        return remote(ref, ref, ss.at[cls, k], rs.at[cls, k], target)

    def got(cls, k, p, kv, ln, rows=None):
        copy(cls, k, p, kv, ln, to_x, rows).wait_recv()

    def sib(k, p, kv, ln):
        ref = full_ref.at[kv, ln, c, p]
        return remote(ref, ref, bs.at[kv, ln, k], br.at[kv, ln, k], to_sib)

    def at(xx, yy):
        return xx * NY + yy

    sent = {
        KX: (0, line, to_x, None),
        KU: (0, line, to_up, None), KD: (0, line, to_down, None),
        VU: (1, line, to_up, None), VD: (1, line, to_down, None),
        K2U: (0, at(ox, y), to_up, None), K2D: (0, at(ox, y), to_down, None),
        KFU: (0, at(xh, down), to_up, 0), KFD: (0, at(xh, up), to_down, 1),
        VFU: (1, at(xh, down), to_up, 0), VFD: (1, at(xh, up), to_down, 1),
        KF2U: (0, at(ox, down), to_up, 0), KF2D: (0, at(ox, up), to_down, 1),
        VX0: (1, line, to_x, None), VX1: (1, at(xh, down), to_x, None),
        VX2: (1, at(xh, up), to_x, None), VX3: (1, at(xh, opp), to_x, None),
    }
    received = {
        KX: (0, at(ox, y), None),
        KU: (0, at(xh, down), None), KD: (0, at(xh, up), None),
        VU: (1, at(xh, down), None), VD: (1, at(xh, up), None),
        K2U: (0, at(ox, down), None), K2D: (0, at(ox, up), None),
        KFU: (0, at(xh, opp), 0), KFD: (0, at(xh, opp), 1),
        VFU: (1, at(xh, opp), 0), VFD: (1, at(xh, opp), 1),
        KF2U: (0, at(ox, opp), 0), KF2D: (0, at(ox, opp), 1),
        VX0: (1, at(ox, y), None), VX1: (1, at(ox, down), None),
        VX2: (1, at(ox, up), None), VX3: (1, at(ox, opp), None),
    }

    def send(cls, k, p):
        kv, ln, target, rows = sent[cls]
        copy(cls, k, p, kv, ln, target, rows).start()

    def wait(cls, k, p):
        kv, ln, rows = received[cls]
        got(cls, k, p, kv, ln, rows)

    @pl.loop(0, NZ + 3)
    def _(step):
        def stage(delay, body):
            k = step - delay

            @pl.when(jnp.logical_and(k >= 0, k < NZ))
            def _():
                body(k, (z + nearest(k) + NZ) % NZ)

        def stage1(k, p):
            for kind in range(2):
                ref = full_ref.at[kind, line, c, p]
                remote(ref, ref, zs.at[kind, 0, 0], zr.at[kind, p], to_x).wait_recv()
            for cls in (KX, KU, KD, VU, VD, VX0):
                send(cls, k, p)
            sib(k, p, 0, line).start()
            sib(k, p, 1, line).start()

        def stage2(k, p):
            wait(KX, k, p)
            send(K2U, k, p)
            send(K2D, k, p)
            wait(KU, k, p)
            send(KFU, k, p)
            wait(KD, k, p)
            send(KFD, k, p)
            wait(VU, k, p)
            send(VFU, k, p)
            send(VX1, k, p)
            wait(VD, k, p)
            send(VFD, k, p)
            send(VX2, k, p)
            sib(k, p, 0, at(ox, y)).start()
            for yy in (down, up):
                sib(k, p, 0, at(xh, yy)).start()
                sib(k, p, 1, at(xh, yy)).start()

        def stage3(k, p):
            wait(K2U, k, p)
            send(KF2U, k, p)
            wait(K2D, k, p)
            send(KF2D, k, p)
            wait(VFU, k, p)
            wait(VFD, k, p)
            send(VX3, k, p)
            wait(KFU, k, p)
            wait(KFD, k, p)
            wait(VX0, k, p)
            sib(k, p, 0, at(xh, opp)).start()
            sib(k, p, 1, at(xh, opp)).start()
            sib(k, p, 0, at(ox, down)).start()
            sib(k, p, 0, at(ox, up)).start()
            sib(k, p, 1, at(ox, y)).start()

        def stage4(k, p):
            wait(KF2U, k, p)
            wait(KF2D, k, p)
            sib(k, p, 0, at(ox, opp)).start()
            for cls, yy in ((VX1, down), (VX2, up), (VX3, opp)):
                wait(cls, k, p)
                sib(k, p, 1, at(ox, yy)).start()

        stage(3, stage4)
        stage(2, stage3)
        stage(1, stage2)
        stage(0, stage1)

    @pl.loop(0, NZ)
    def _(k):
        p = (z + nearest(k) + NZ) % NZ
        remote(qr_ref.at[p], qr_ref.at[p], zs.at[2, 0, 0], zr.at[2, p], to_x).wait_recv()
        z_each(k, (0, 1, 2), lambda d: d.wait_send(), None)
        for cls in range(NCLASS):
            kv, ln, target, rows = sent[cls]
            copy(cls, k, p, kv, ln, target, rows).wait_send()

        @pl.loop(0, LINES)
        def _(ln):
            for kv in range(2):
                sib(k, p, kv, ln).wait_send()
                other = full_ref.at[kv, ln, 1 - c, p]
                remote(other, other, bs.at[kv, ln, k], br.at[kv, ln, k], to_sib).wait_recv()


def gather_call(queries, keys_values):
    anyspace = pl.BlockSpec(memory_space=pl.ANY)
    return pl.pallas_call(
        gather_kernel,
        out_shape=(
            jax.ShapeDtypeStruct((2, LINES, NC, NZ, HALF, HEAD_DIM), jnp.bfloat16),
            jax.ShapeDtypeStruct((NZ, HALF, HEAD_DIM), jnp.bfloat16),
        ),
        in_specs=[anyspace, anyspace],
        out_specs=(anyspace, anyspace),
        scratch_shapes=[
            pltpu.SemaphoreType.DMA((3, NC, NZ)),
            pltpu.SemaphoreType.DMA((3, NZ)),
            pltpu.SemaphoreType.DMA((NCLASS, NZ)),
            pltpu.SemaphoreType.DMA((NCLASS, NZ)),
            pltpu.SemaphoreType.DMA((2, LINES, NZ)),
            pltpu.SemaphoreType.DMA((2, LINES, NZ)),
        ],
        compiler_params=pltpu.CompilerParams(collective_id=1, has_side_effects=True),
        name="gather_keys_values",
    )(queries, keys_values)


AHEAD = 16
SCALE = math.log2(math.e) / HEAD_DIM**0.5


def attend_kernel(meta, rand, q_ref, full_ref, o_ref, near, glob, far, near_sem, edge_sem, glob_sem, far_sem):
    line, c = meta[0], meta[1]

    def near_copy(kv, zz, half):
        src = full_ref.at[kv, pl.ds(((line * NC + half) * NZ + zz) * HALF_BLOCKS, HALF_BLOCKS)]
        dst = near.at[kv, pl.ds(1 + zz * SHARD_BLOCKS + half * HALF_BLOCKS, HALF_BLOCKS)]
        return pltpu.make_async_copy(src, dst, near_sem.at[kv, zz, half])

    def edge_copy(kv, side):
        return pltpu.make_async_copy(
            full_ref.at[kv, meta[2 + side]], near.at[kv, side * (LINE_BLOCKS + 1)], edge_sem.at[kv, side]
        )

    def glob_copy(kv, g):
        return pltpu.make_async_copy(full_ref.at[kv, meta[4 + g]], glob.at[kv, g], glob_sem.at[kv, g])

    def far_start(n):
        for kv in range(2):
            for r in range(NRANDOM):
                pltpu.make_async_copy(
                    full_ref.at[kv, rand[n * NRANDOM + r]], far.at[n, kv, r], far_sem.at[n]
                ).start()

    for kv in range(2):
        for i in range(2):
            glob_copy(kv, i).start()
            edge_copy(kv, i).start()

    @pl.loop(0, NZ)
    def _(zz):
        for kv in range(2):
            for half in range(NC):
                near_copy(kv, zz, half).start()

    @pl.loop(0, AHEAD)
    def _(n):
        far_start(n)

    for kv in range(2):
        for i in range(2):
            glob_copy(kv, i).wait()
            edge_copy(kv, i).wait()

    @pl.loop(0, NZ)
    def _(zz):
        for kv in range(2):
            for half in range(NC):
                near_copy(kv, zz, half).wait()

    column = lax.broadcasted_iota(jnp.int32, (1, 512), 1)

    def one(n):
        pltpu.make_async_copy(far.at[n], far.at[n], far_sem.at[n]).wait()

        @pl.when(n + AHEAD < Q_BLOCKS)
        def _():
            far_start(n + AHEAD)

        middle = (n // HALF_BLOCKS) * SHARD_BLOCKS + c * HALF_BLOCKS + n % HALF_BLOCKS
        block = line * LINE_BLOCKS + middle
        first = jnp.logical_and(block == 0, column < BLOCK)
        last = jnp.logical_and(
            block == LINES * LINE_BLOCKS - 1, jnp.logical_and(column >= 2 * BLOCK, column < 3 * BLOCK)
        )
        bias = jnp.where(jnp.logical_or(first, last), -jnp.inf, 0.0).astype(jnp.float32)

        def listed(kv):
            return jnp.concatenate(
                [
                    near[kv, pl.ds(middle, 3)].reshape(3 * BLOCK, HEAD_DIM),
                    far[n, kv].reshape(NRANDOM * BLOCK, HEAD_DIM),
                    glob[kv].reshape(NGLOBAL * BLOCK, HEAD_DIM),
                ],
                axis=0,
            )

        scores = lax.dot_general(
            q_ref[n], listed(0), (((1,), (1,)), ((), ())), preferred_element_type=jnp.float32
        )
        scores = scores * SCALE + bias
        highest = jnp.max(scores, axis=1, keepdims=True)
        weights = jnp.exp2(scores - highest)
        total = jnp.sum(weights, axis=1, keepdims=True)
        mixed = jnp.dot(weights.astype(jnp.bfloat16), listed(1), preferred_element_type=jnp.float32)
        o_ref[n] = (mixed / total).astype(jnp.bfloat16)

    @pl.loop(0, Q_BLOCKS // 4)
    def _(m):
        for u in range(4):
            one(m * 4 + u)


def attend_call(meta, rand, q, full):
    whole = pl.BlockSpec(memory_space=pltpu.VMEM)
    smem = pl.BlockSpec(memory_space=pltpu.SMEM)
    return pl.pallas_call(
        attend_kernel,
        out_shape=jax.ShapeDtypeStruct((Q_BLOCKS, BLOCK, HEAD_DIM), jnp.bfloat16),
        in_specs=[smem, smem, whole, pl.BlockSpec(memory_space=pl.ANY)],
        out_specs=whole,
        scratch_shapes=[
            pltpu.VMEM((2, LINE_BLOCKS + 2, BLOCK, HEAD_DIM), jnp.bfloat16),
            pltpu.VMEM((2, NGLOBAL, BLOCK, HEAD_DIM), jnp.bfloat16),
            pltpu.VMEM((Q_BLOCKS, 2, NRANDOM, BLOCK, HEAD_DIM), jnp.bfloat16),
            pltpu.SemaphoreType.DMA((2, NZ, NC)),
            pltpu.SemaphoreType.DMA((2, 2)),
            pltpu.SemaphoreType.DMA((2, NGLOBAL)),
            pltpu.SemaphoreType.DMA((Q_BLOCKS,)),
        ],
        compiler_params=pltpu.CompilerParams(vmem_limit_bytes=48 * 1024 * 1024),
        name="attend",
    )(meta, rand, q, full)


def return_kernel(a_ref, out_ref, zs, zr, ss, rs):
    xh, y, z, xl, c = coords()
    to_lo, to_sib = device(xh, y, z, 1 - xl, c), device(xh, y, z, xl, 1 - c)
    barrier = pltpu.get_barrier_semaphore()
    friends = [device(xh, y, (z + dz) % NZ, xl, c) for dz in range(1, NZ)] + [to_lo, to_sib]
    for friend in friends:
        pl.semaphore_signal(barrier, inc=1, device_id=friend, device_id_type=MESH)
    pl.semaphore_wait(barrier, len(friends))

    def place(half, side, plane):
        cols = pl.ds(pl.multiple_of((side * NZ + plane) * HEAD_DIM, HEAD_DIM), HEAD_DIM)
        return out_ref.at[pl.ds(pl.multiple_of(half * HALF, HALF), HALF), cols]

    def z_copy(k):
        t = (z + nearest(k) + NZ) % NZ
        return remote(a_ref.at[t], place(c, xl, z), zs.at[k], zr.at[z], device(xh, y, t, xl, c))

    def own():
        return pltpu.make_async_copy(a_ref.at[z], place(c, xl, z), zr.at[z])

    own().start()

    @pl.loop(1, NZ)
    def _(k):
        z_copy(k).start()

    def copy(cls, k, half, side, p, target):
        ref = place(half, side, p)
        return remote(ref, ref, ss.at[cls, k], rs.at[cls, k], target)

    @pl.loop(0, NZ + 1)
    def _(step):
        @pl.when(step > 0)
        def _():
            k = step - 1
            p = (z + nearest(k) + NZ) % NZ
            copy(0, k, c, 1 - xl, p, to_lo).wait_recv()
            copy(2, k, c, 1 - xl, p, to_sib).start()

        @pl.when(step < NZ)
        def _():
            p = (z + nearest(step) + NZ) % NZ
            remote(place(c, xl, p), place(c, xl, p), zs.at[0], zr.at[p], to_lo).wait_recv()
            copy(0, step, c, xl, p, to_lo).start()
            copy(1, step, c, xl, p, to_sib).start()

    @pl.loop(0, NZ)
    def _(k):
        p = (z + nearest(k) + NZ) % NZ

        @pl.when(k > 0)
        def _():
            z_copy(k).wait_send()

        copy(0, k, c, xl, p, to_lo).wait_send()
        copy(1, k, c, xl, p, to_sib).wait_send()
        copy(2, k, c, 1 - xl, p, to_sib).wait_send()
        copy(1, k, 1 - c, xl, p, to_sib).wait_recv()
        copy(2, k, 1 - c, 1 - xl, p, to_sib).wait_recv()


def return_call(attended):
    anyspace = pl.BlockSpec(memory_space=pl.ANY)
    return pl.pallas_call(
        return_kernel,
        out_shape=jax.ShapeDtypeStruct((ROWS, NXL * NZ * HEAD_DIM), jnp.bfloat16),
        in_specs=[anyspace],
        out_specs=anyspace,
        scratch_shapes=[
            pltpu.SemaphoreType.DMA((NZ,)),
            pltpu.SemaphoreType.DMA((NZ,)),
            pltpu.SemaphoreType.DMA((3, NZ)),
            pltpu.SemaphoreType.DMA((3, NZ)),
        ],
        compiler_params=pltpu.CompilerParams(collective_id=2, has_side_effects=True),
        name="return_attended",
    )(attended)


def address(block):
    shard, offset = block // SHARD_BLOCKS, block % SHARD_BLOCKS
    line, plane = shard // NZ, shard % NZ
    return ((line * NC + offset // HALF_BLOCKS) * NZ + plane) * HALF_BLOCKS + offset % HALF_BLOCKS


def body(queries, keys_values, global_ids, rand_ids, out_weight):
    xh, y, z, xl, c = coords()
    line = xh * NY + y
    total = LINES * LINE_BLOCKS
    lists = rand_ids.reshape(LINES, NZ, NC, HALF_BLOCKS * NRANDOM)
    mine = lax.dynamic_slice(lists, (line, 0, c, 0), (1, NZ, 1, HALF_BLOCKS * NRANDOM)).reshape(-1)
    rand = address(mine)
    edges = jnp.stack([line * LINE_BLOCKS - 1, line * LINE_BLOCKS + LINE_BLOCKS])
    blocks = jnp.concatenate([jnp.clip(edges, 0, total - 1), global_ids])
    meta = jnp.concatenate([jnp.stack([line, c]), address(blocks)])

    full, q = gather_call(queries, keys_values)
    full = full.reshape(2, total, BLOCK, HEAD_DIM)
    attended = attend_call(meta, rand, q.reshape(Q_BLOCKS, BLOCK, HEAD_DIM), full)
    everything = return_call(attended.reshape(NZ, HALF, HEAD_DIM))
    summed = jnp.dot(everything, out_weight, preferred_element_type=jnp.float32)
    return summed.astype(jnp.bfloat16)


def solution(mesh):
    in_specs = (P("seq", "head"), P(None, "seq", "head"), P(), P(), P(None, "head"))
    return jax.shard_map(body, mesh=mesh, in_specs=in_specs, out_specs=P("seq", "head"), check_vma=False)
```

time: 1350 us -> 333 us (0.25)
  waiting for transfers between devices: 1060 us -> 0 us
  Pallas kernels: 0 us -> 313 us
  local copies, waits for them, and re-layouts: 132 us -> 4.08 us
  other arithmetic: 63.6 us -> 1.03 us
  starting transfers between devices: 44.5 us -> 0 us
  matrix products: 31.4 us -> 11.1 us
  between operations: 17.4 us -> 0.07 us
    psum x1 -> x0, waiting for transfers between devices: 447 us -> none  [broadcast(): return lax.psum(block, axis)]
    all_to_all x3 -> x0, waiting for transfers between devices: 341 us -> none  [body(): lax.all_to_all(outgoing, 'seq', split_axis=1, concat_axis=1, tiled=True)]
    pallas_call x0 -> x3, Pallas kernels: none -> 313 us  [the longest x1 200 us: gather_call(): pl.pallas_call(gather_kernel, out_shape=(jax.ShapeDtypeStruct((2, LINES,...]
    ppermute x2 -> x0, waiting for transfers between devices: 171 us -> none  [the longest x1 171 us: padded_2(): lax.ppermute(lax.slice_in_dim(block, block.shape[dim] - width, None, axis...]
    all_gather x1 -> x0, waiting for transfers between devices: 99.9 us -> none  [body(): lax.all_gather(attended, 'head', axis=1, tiled=True)]
    slice x15 -> x0, local copies, waits for them, and re-layouts: 42.1 us -> none  [the longest x6 20.3 us: one_group(): local[0]]
    all_to_all x3 -> x0, starting transfers between devices: 38.1 us -> none  [body(): lax.all_to_all(outgoing, 'seq', split_axis=1, concat_axis=1, tiled=True)]
    gather x6 -> x0, local copies, waits for them, and re-layouts: 35.8 us -> none  [the longest x3 18.1 us: body(): outgoing = jnp.take(pair_blocks, chosen, axis=1)]
  transfers between devices with their start and end apart: 7 -> 0, of which waited for: 5 -> 0; matrix products, arithmetic and copies ran while one was open for 5% -> 0% of each run, Pallas kernels for 0% -> 0%
where the time goes in v1:
time: 333 us; the launch traced here: 329 us
  Pallas kernels  313 us (94%)
  matrix products  11.1 us (3%)
  local copies, waits for them, and re-layouts  4.08 us (1%)
    pallas_call x1, Pallas kernels, gather_call(): pl.pallas_call(gather_kernel, out_shape=(jax.ShapeDtypeStruct((2, LINES,...  200 us
    pallas_call x1, Pallas kernels, return_call(): pl.pallas_call(return_kernel, out_shape=jax.ShapeDtypeStruct((ROWS, NXL *...  68.3 us
    pallas_call x1, Pallas kernels, attend_call(): pl.pallas_call(attend_kernel, out_shape=jax.ShapeDtypeStruct((Q_BLOCKS, B...  43.9 us
    dot_general x1, matrix products, body(): summed = jnp.dot(everything, out_weight, preferred_element_type=jnp.float32)  11.1 us

profile of v1, /device:TPU:97, one launch (start us, length us, event | category | flops | bytes accessed | tf_op | source)
XLA Modules:
  0.0 328.9 jit_solution(11298316574226790084)
XLA Ops:
  0.0 0.1 add_clamp_fusion
  0.1 0.8 fusion.9
  0.8 0.1 pad_add_fusion.1.meta
  0.9 1.0 copy.6
  1.9 0.3 reshape.20
  2.3 0.1 ne.123
  2.4 0.1 div.71
  2.5 0.1 rem.168
  2.6 200.4 %gather_keys_values.1 = (bf16[2,8,2,8,768,128]{5,4,3,2,1,0:T(8,128)(2,1)}, bf16[8,768,128]{2,1,0:T(8,128)(2,1)}) custom-call(bf16[1536,512]{1,0:T(8,128)(2,1)} %q_ref.1, bf16[2,1536,512]{2,1,0:T(8,128)(2,1)} %kv_ref.1), custom_call_target="tpu_custom_call" | custom-call | tf_op jit(solution)/shard_map/gather_keys_values/pallas_call | solution.py:240
  203.0 0.0 copy-start.1
  203.0 1.4 copy-done.1
  204.4 43.9 %attend.1 = bf16[96,64,128]{2,1,0:T(8,128)(2,1)S(1)} custom-call(s32[6]{0:T(128)S(1)} %pad_add_fusion.1.meta, s32[288]{0:T(512)S(1)} %fusion.4.rand, bf16[96,64,128]{2,1,0:T(8,128)(2,1)S(1)} %bitcast.10, bf16[2,1536,64,128]{3,2,1,0:T(8,128)(2,1)} %bitcast.11), custom_call_target="tpu_custom_call" | custom-call | tf_op jit(solution)/shard_map/attend/pallas_call | solution.py:360
  248.4 0.0 copy-start
  248.4 1.1 copy-done
  249.5 68.3 %return_attended.1 = bf16[1536,2048]{1,0:T(8,128)(2,1)} custom-call(bf16[8,768,128]{2,1,0:T(8,128)(2,1)} %bitcast.9), custom_call_target="tpu_custom_call" | custom-call | tf_op jit(solution)/shard_map/return_attended/pallas_call | solution.py:442
  317.8 11.1 %convolution_convert_fusion = bf16[1536,1024]{1,0:T(8,128)(2,1)} fusion(bf16[1536,2048]{1,0:T(8,128)(2,1)} %return_attended.1, bf16[2048,1024]{1,0:T(8,128)(2,1)} %param.9), kind=kOutput, calls=%fused_computation | convolution fusion | flops 6444023808 | bytes 13631488 | tf_op jit(solution)/shard_map/dot_general | solution.py:479
  (3 shorter events, 0.1 us)
Async XLA Ops:
  203.0 1.4 copy-start.1
  248.4 1.1 copy-start

commit v2 on v0

v2 whole, which is shorter than its diff:
```python
import math

import jax
import jax.numpy as jnp
from jax import lax
from jax.experimental import pallas as pl
from jax.experimental.pallas import tpu as pltpu
from jax.sharding import PartitionSpec as P

HEAD_DIM = 128
BLOCK = 64
NGLOBAL = 2
NRANDOM = 3
MESH = pl.DeviceIdType.MESH

NXH, NY, NZ, NXL, NC = 2, 4, 8, 2, 2
LINES = NXH * NY
SHARD_BLOCKS = 24
ROWS = SHARD_BLOCKS * BLOCK
HALF_BLOCKS = SHARD_BLOCKS // NC
HALF = HALF_BLOCKS * BLOCK
LINE_BLOCKS = NZ * SHARD_BLOCKS
Q_BLOCKS = NZ * HALF_BLOCKS


def coords():
    seq = lax.axis_index("seq")
    head = lax.axis_index("head")
    return seq // (NY * NZ), (seq // NZ) % NY, seq % NZ, head // NC, head % NC


def device(xh, y, z, xl, c):
    return ((xh * NY + y) * NZ + z, xl * NC + c)


def remote(src, dst, send_sem, recv_sem, target):
    return pltpu.make_async_remote_copy(
        src_ref=src, dst_ref=dst, send_sem=send_sem, recv_sem=recv_sem,
        device_id=target, device_id_type=MESH,
    )


def nearest(k):
    return (k % 2) * ((k + 1) // 2) - (1 - k % 2) * (k // 2)


X0, U1, D1, U2, D2, FU, FD, F2, G2 = range(9)
NCLASS = 9
ITEMS = 2 * NZ
SCORES_FROM = NZ + 3
SCALE = math.log2(math.e) / HEAD_DIM**0.5


def address(block):
    shard, offset = block // SHARD_BLOCKS, block % SHARD_BLOCKS
    line, plane = shard // NZ, shard % NZ
    return ((line * NC + offset // HALF_BLOCKS) * NZ + plane) * HALF_BLOCKS + offset % HALF_BLOCKS


def attention_kernel(table, q_ref, kv_ref, out_ref, kbuf, vbuf, qbuf, pbuf, obuf, zs, zr, cs, cr, bs, br, rzs, rzr, ras, rar):
    xh, y, z, xl, c = coords()
    line = xh * NY + y
    up, down, opp = (y + 1) % NY, (y + NY - 1) % NY, (y + 2) % NY
    ox = 1 - xh
    to_x, to_up, to_down = device(ox, y, z, xl, c), device(xh, up, z, xl, c), device(xh, down, z, xl, c)
    to_sib, to_lo = device(xh, y, z, xl, 1 - c), device(xh, y, z, 1 - xl, c)
    bufs = (kbuf, vbuf)

    barrier = pltpu.get_barrier_semaphore()
    friends = [
        device(xh, y, (z + dz) % NZ, xl, (c + dc) % NC)
        for dz in range(NZ) for dc in range(NC) if dz or dc
    ] + [to_x, to_up, to_down, to_lo]
    for friend in friends:
        pl.semaphore_signal(barrier, inc=1, device_id=friend, device_id_type=MESH)
    pl.semaphore_wait(barrier, len(friends))

    def piece(kv, ln, half, p):
        return bufs[kv].at[pl.ds(((ln * NC + half) * NZ + p) * HALF_BLOCKS, HALF_BLOCKS)]

    def near_plane(k):
        return (z + nearest(k) + NZ) % NZ

    def z_parts(t, kind, half):
        cols = pl.ds(pl.multiple_of((t - 4 * c) * HEAD_DIM, HEAD_DIM), HEAD_DIM)
        rows = pl.ds(half * HALF_BLOCKS, HALF_BLOCKS)
        if kind == 2:
            return q_ref.at[rows, :, cols], qbuf.at[pl.ds(z * HALF_BLOCKS, HALF_BLOCKS)]
        return kv_ref.at[kind, rows, :, cols], piece(kind, line, half, z)

    def z_each(k, kind, remote_fn, local_fn):
        t = near_plane(k)

        @pl.when(t // 4 == c)
        def _():
            for half in range(NC):
                src, dst = z_parts(t, kind, half)
                mine = jnp.logical_and(t == z, c == half)
                if local_fn is not None:
                    @pl.when(mine)
                    def _():
                        local_fn(pltpu.make_async_copy(src, dst, zr.at[kind, z]))

                @pl.when(jnp.logical_not(mine))
                def _():
                    remote_fn(remote(src, dst, zs.at[kind, half, k], zr.at[kind, z], device(xh, y, t, xl, half)))

    for kind in (0, 2, 1):
        @pl.loop(0, NZ)
        def _(k):
            z_each(k, kind, lambda d: d.start(), lambda d: d.start())

    H = HALF_BLOCKS // 2

    def at(xx, yy):
        return xx * NY + yy

    def copy(cls, e, p, kv, ln, target, rows=None):
        ref = piece(kv, ln, c, p)
        if rows is not None:
            ref = ref.at[pl.ds(rows * H, H)]
        return remote(ref, ref, cs.at[cls, e], cr.at[cls, e], target)

    def sib(e, p, kv, ln, half):
        ref = piece(kv, ln, half, p)
        return remote(ref, ref, bs.at[e, ln], br.at[e, ln], to_sib)

    shared = {
        U1: (at(xh, y), to_up, None, at(xh, down)), D1: (at(xh, y), to_down, None, at(xh, up)),
        X0: (at(xh, y), to_x, None, at(ox, y)),
        FU: (at(xh, down), to_up, 0, at(xh, opp)), FD: (at(xh, up), to_down, 1, at(xh, opp)),
    }
    x_first = dict(shared)
    x_first.update({
        U2: (at(ox, y), to_up, None, at(ox, down)), D2: (at(ox, y), to_down, None, at(ox, up)),
        F2: (at(ox, down), to_up, 0, at(ox, opp)), G2: (at(ox, up), to_down, 1, at(ox, opp)),
    })
    y_first = dict(shared)
    y_first.update({
        U2: (at(xh, down), to_x, None, at(ox, down)), D2: (at(xh, up), to_x, None, at(ox, up)),
        F2: (at(xh, opp), to_x, None, at(ox, opp)),
    })

    def is_x_first(kv, k):
        even = k % 2 == 0
        return even if kv == 0 else jnp.logical_or(even, k == NZ - 1)

    def modes(kv, k, body):
        first = is_x_first(kv, k)

        @pl.when(first)
        def _():
            body(x_first, True)

        @pl.when(jnp.logical_not(first))
        def _():
            body(y_first, False)

    def stages(kv, k, p, classes, xf, stage):
        e = kv * NZ + k

        def send(cls):
            ln, target, rows, _ = classes[cls]
            copy(cls, e, p, kv, ln, target, rows).start()

        def wait(cls):
            _, target, rows, ln = classes[cls]
            copy(cls, e, p, kv, ln, target, rows).wait_recv()

        def share(ln):
            sib(e, p, kv, ln, c).start()

        if stage == 1:
            ref = piece(kv, line, c, p)
            remote(ref, ref, zs.at[kv, 0, 0], zr.at[kv, p], to_x).wait_recv()
            for cls in (X0, U1, D1):
                send(cls)
            share(line)
        elif stage == 2 and xf:
            wait(X0)
            send(U2)
            send(D2)
            wait(U1)
            send(FU)
            wait(D1)
            send(FD)
            for ln in (at(ox, y), at(xh, down), at(xh, up)):
                share(ln)
        elif stage == 2:
            wait(U1)
            send(U2)
            send(FU)
            wait(D1)
            send(D2)
            send(FD)
            for ln in (at(xh, down), at(xh, up)):
                share(ln)
        elif stage == 3 and xf:
            wait(U2)
            send(F2)
            wait(D2)
            send(G2)
            wait(FU)
            wait(FD)
            for ln in (at(ox, down), at(ox, up), at(xh, opp)):
                share(ln)
        elif stage == 3:
            wait(FU)
            wait(FD)
            send(F2)
            wait(X0)
            for ln in (at(xh, opp), at(ox, y)):
                share(ln)
        elif xf:
            wait(F2)
            wait(G2)
            share(at(ox, opp))
        else:
            for cls, yy in ((U2, down), (D2, up), (F2, opp)):
                wait(cls)
                share(at(ox, yy))

    def sib_received(kv):
        @pl.loop(0, NZ)
        def _(k):
            p = near_plane(k)

            @pl.loop(0, LINES)
            def _(ln):
                sib(kv * NZ + k, p, kv, ln, 1 - c).wait_recv()

    column = lax.broadcasted_iota(jnp.int32, (1, 512), 1)
    globals_at = Q_BLOCKS * NRANDOM

    def listed(buf, n, block):
        last_block = LINES * LINE_BLOCKS - 1
        spots = [
            address(jnp.maximum(block - 1, 0)), address(block), address(jnp.minimum(block + 1, last_block)),
        ] + [table[n * NRANDOM + r] for r in range(NRANDOM)] + [table[globals_at + g] for g in range(NGLOBAL)]
        return jnp.concatenate([buf[s] for s in spots], axis=0)

    def doc_block(plane, o):
        return line * LINE_BLOCKS + plane * SHARD_BLOCKS + c * HALF_BLOCKS + o

    def weigh(plane, o):
        n, block = plane * HALF_BLOCKS + o, doc_block(plane, o)
        first = jnp.logical_and(block == 0, column < BLOCK)
        last = jnp.logical_and(
            block == LINES * LINE_BLOCKS - 1, jnp.logical_and(column >= 2 * BLOCK, column < 3 * BLOCK)
        )
        bias = jnp.where(jnp.logical_or(first, last), -jnp.inf, 0.0).astype(jnp.float32)
        scores = lax.dot_general(
            qbuf[n], listed(kbuf, n, block), (((1,), (1,)), ((), ())), preferred_element_type=jnp.float32
        )
        scores = scores * SCALE + bias
        powers = jnp.exp2(scores - jnp.max(scores, axis=1, keepdims=True))
        pbuf[n] = (powers * (1.0 / jnp.sum(powers, axis=1, keepdims=True))).astype(jnp.bfloat16)

    def mix(plane, o):
        n, block = plane * HALF_BLOCKS + o, doc_block(plane, o)
        mixed = jnp.dot(pbuf[n], listed(vbuf, n, block), preferred_element_type=jnp.float32)
        obuf[n] = mixed.astype(jnp.bfloat16)

    def blocks_of(plane, fn):
        @pl.loop(0, HALF_BLOCKS // 4)
        def _(m):
            for u in range(4):
                fn(plane, m * 4 + u)

    @pl.loop(0, ITEMS + 3)
    def _(step):
        for stage in (4, 3, 2, 1):
            e = step - (stage - 1)
            for kv in range(2):
                @pl.when(jnp.logical_and(e >= kv * NZ, e < (kv + 1) * NZ))
                def _():
                    k = e - kv * NZ
                    p = near_plane(k)
                    modes(kv, k, lambda classes, xf: stages(kv, k, p, classes, xf, stage))

        @pl.when(step == SCORES_FROM)
        def _():
            sib_received(0)

            @pl.loop(0, NZ)
            def _(p):
                ref = qbuf.at[pl.ds(p * HALF_BLOCKS, HALF_BLOCKS)]
                remote(ref, ref, zs.at[2, 0, 0], zr.at[2, p], to_x).wait_recv()

        @pl.when(step >= SCORES_FROM)
        def _():
            blocks_of(step - SCORES_FROM, weigh)

    sib_received(1)

    def place(half, side, plane):
        cols = pl.ds(pl.multiple_of((side * NZ + plane) * HEAD_DIM, HEAD_DIM), HEAD_DIM)
        return out_ref.at[pl.ds(half * HALF_BLOCKS, HALF_BLOCKS), :, cols]

    def rows_of(p):
        return obuf.at[pl.ds(p * HALF_BLOCKS, HALF_BLOCKS)]

    def home(k, p):
        return remote(rows_of(p), place(c, xl, z), rzs.at[k], rzr.at[z], device(xh, y, p, xl, c))

    def onward(cls, k, half, side, p, target):
        ref = place(half, side, p)
        return remote(ref, ref, ras.at[cls, k], rar.at[cls, k], target)

    @pl.loop(0, NZ + 4)
    def _(step):
        @pl.when(step < NZ)
        def _():
            p = near_plane(step)
            blocks_of(p, mix)

            @pl.when(step == 0)
            def _():
                pltpu.make_async_copy(rows_of(z), place(c, xl, z), rzr.at[z]).start()

            @pl.when(step > 0)
            def _():
                home(step, p).start()

        @pl.when(jnp.logical_and(step >= 2, step < NZ + 2))
        def _():
            k = step - 2
            p = near_plane(k)
            remote(place(c, xl, p), place(c, xl, p), rzs.at[0], rzr.at[p], to_lo).wait_recv()
            onward(0, k, c, xl, p, to_lo).start()
            onward(1, k, c, xl, p, to_sib).start()

        @pl.when(step >= 4)
        def _():
            k = step - 4
            p = near_plane(k)
            onward(0, k, c, 1 - xl, p, to_lo).wait_recv()
            onward(2, k, c, 1 - xl, p, to_sib).start()

    @pl.loop(0, NZ)
    def _(k):
        p = near_plane(k)

        @pl.when(k > 0)
        def _():
            home(k, p).wait_send()

        onward(0, k, c, xl, p, to_lo).wait_send()
        onward(1, k, c, xl, p, to_sib).wait_send()
        onward(2, k, c, 1 - xl, p, to_sib).wait_send()
        onward(1, k, 1 - c, xl, p, to_sib).wait_recv()
        onward(2, k, 1 - c, 1 - xl, p, to_sib).wait_recv()
        for kind in range(3):
            z_each(k, kind, lambda d: d.wait_send(), None)
        for kv in range(2):
            e = kv * NZ + k

            def sent(classes, xf):
                for cls, (ln, target, rows, _) in classes.items():
                    copy(cls, e, p, kv, ln, target, rows).wait_send()

            modes(kv, k, sent)

            @pl.loop(0, LINES)
            def _(ln):
                sib(e, p, kv, ln, c).wait_send()


def attention_call(table, queries, keys_values):
    anyspace = pl.BlockSpec(memory_space=pl.ANY)
    dma = pltpu.SemaphoreType.DMA
    key_blocks = LINES * LINE_BLOCKS
    return pl.pallas_call(
        attention_kernel,
        out_shape=jax.ShapeDtypeStruct((SHARD_BLOCKS, BLOCK, NXL * NZ * HEAD_DIM), jnp.bfloat16),
        in_specs=[pl.BlockSpec(memory_space=pltpu.SMEM), anyspace, anyspace],
        out_specs=anyspace,
        scratch_shapes=[
            pltpu.VMEM((key_blocks, BLOCK, HEAD_DIM), jnp.bfloat16),
            pltpu.VMEM((key_blocks, BLOCK, HEAD_DIM), jnp.bfloat16),
            pltpu.VMEM((Q_BLOCKS, BLOCK, HEAD_DIM), jnp.bfloat16),
            pltpu.VMEM((Q_BLOCKS, BLOCK, 512), jnp.bfloat16),
            pltpu.VMEM((Q_BLOCKS, BLOCK, HEAD_DIM), jnp.bfloat16),
            dma((3, NC, NZ)), dma((3, NZ)),
            dma((NCLASS, ITEMS)), dma((NCLASS, ITEMS)),
            dma((ITEMS, LINES)), dma((ITEMS, LINES)),
            dma((NZ,)), dma((NZ,)), dma((3, NZ)), dma((3, NZ)),
        ],
        compiler_params=pltpu.CompilerParams(
            collective_id=1, has_side_effects=True, vmem_limit_bytes=60 * 1024 * 1024
        ),
        name="block_attention",
    )(table, queries, keys_values)


def body(queries, keys_values, global_ids, rand_ids, out_weight):
    xh, y, z, xl, c = coords()
    width = queries.shape[1]
    lists = rand_ids.reshape(LINES, NZ, NC, HALF_BLOCKS * NRANDOM)
    mine = lax.dynamic_slice(lists, (xh * NY + y, 0, c, 0), (1, NZ, 1, HALF_BLOCKS * NRANDOM)).reshape(-1)
    table = address(jnp.concatenate([mine, global_ids]))
    attended = attention_call(
        table,
        queries.reshape(SHARD_BLOCKS, BLOCK, width),
        keys_values.reshape(2, SHARD_BLOCKS, BLOCK, width),
    )
    summed = jnp.dot(attended.reshape(ROWS, -1), out_weight, preferred_element_type=jnp.float32)
    return summed.astype(jnp.bfloat16)


def solution(mesh):
    in_specs = (P("seq", "head"), P(None, "seq", "head"), P(), P(), P(None, "head"))
    return jax.shard_map(body, mesh=mesh, in_specs=in_specs, out_specs=P("seq", "head"), check_vma=False)
```

time: 1350 us -> 308 us (0.23)
  the two profiles are of different devices: /device:TPU:97 before, /device:TPU:227 now
where the time goes in v2:
time: 308 us
  Pallas kernels  294 us (95%)
  matrix products  11.1 us (4%)
    pallas_call x1, Pallas kernels, attention_call(): pl.pallas_call(attention_kernel, out_shape=jax.ShapeDtypeStruct((SHARD_BL...  294 us
    dot_general x1, matrix products, body(): jnp.dot(attended.reshape(ROWS, -1), out_weight, preferred_element_type=jn...  11.1 us

profile of v2, /device:TPU:227, one launch (start us, length us, event | category | flops | bytes accessed | tf_op | source)
XLA Modules:
  0.0 308.1 jit_solution(8108551654265206109)
XLA Ops:
  0.0 1.0 copy.6
  1.0 0.3 reshape.15
  1.3 0.1 reshape.16
  1.4 1.3 fusion.4.table
  2.8 294.2 %block_attention.1 = bf16[24,64,2048]{2,1,0:T(8,128)(2,1)} custom-call(s32[290]{0:T(512)} %fusion.4.table, bf16[24,64,512]{2,1,0:T(8,128)(2,1)} %bitcast.7, bf16[2,24,64,512]{3,2,1,0:T(8,128)(2,1)} %bitcast.6), custom_call_target="tpu_custom_call" | custom-call | tf_op jit(solution)/shard_map/block_attention/pallas_call | solution.py:373
  296.9 11.1 %convolution_convert_fusion = bf16[1536,1024]{1,0:T(8,128)(2,1)} fusion(bf16[1536,2048]{1,0:T(8,128)(2,1)} %bitcast.5, bf16[2048,1024]{1,0:T(8,128)(2,1)} %param.9), kind=kOutput, calls=%fused_computation | convolution fusion | flops 6444023808 | bytes 13631488 | tf_op jit(solution)/shard_map/dot_general | solution.py:407
  (1 shorter events, 0.0 us)

commit v3 on v2

--- a/solution.py
+++ b/solution.py
@@ -44,10 +44,13 @@
     return (k % 2) * ((k + 1) // 2) - (1 - k % 2) * (k // 2)
 
 
-X0, U1, D1, U2, D2, FU, FD, F2, G2 = range(9)
-NCLASS = 9
+X0, U1, D1, U2, D2, FU, FD, YU, YD, F2, G2, YO = range(12)
+NCLASS = 12
+FROM_X = (7, 6)
+Z_LEAD = 2
 ITEMS = 2 * NZ
-SCORES_FROM = NZ + 3
+DELAY = (0, 0, 2, 4, 6)
+SCORES_FROM = NZ + DELAY[4]
 SCALE = math.log2(math.e) / HEAD_DIM**0.5
 
 
@@ -105,120 +108,89 @@
                 def _():
                     remote_fn(remote(src, dst, zs.at[kind, half, k], zr.at[kind, z], device(xh, y, t, xl, half)))
 
-    for kind in (0, 2, 1):
-        @pl.loop(0, NZ)
-        def _(k):
-            z_each(k, kind, lambda d: d.start(), lambda d: d.start())
+    def z_start(k, kind):
+        z_each(k, kind, lambda d: d.start(), lambda d: d.start())
+
+    @pl.loop(0, Z_LEAD)
+    def _(k):
+        z_start(k, 0)
 
     H = HALF_BLOCKS // 2
 
     def at(xx, yy):
         return xx * NY + yy
 
-    def copy(cls, e, p, kv, ln, target, rows=None):
-        ref = piece(kv, ln, c, p)
-        if rows is not None:
-            ref = ref.at[pl.ds(rows * H, H)]
+    def routes(kv):
+        m = FROM_X[kv]
+        h = (m + 1) // 2
+        rest = (m, HALF_BLOCKS - m)
+        return {
+            X0: (line, to_x, (0, HALF_BLOCKS), at(ox, y)),
+            U1: (line, to_up, (0, HALF_BLOCKS), at(xh, down)),
+            D1: (line, to_down, (0, HALF_BLOCKS), at(xh, up)),
+            U2: (at(ox, y), to_up, (0, m), at(ox, down)),
+            D2: (at(ox, y), to_down, (0, m), at(ox, up)),
+            FU: (at(xh, down), to_up, (0, H), at(xh, opp)),
+            FD: (at(xh, up), to_down, (H, H), at(xh, opp)),
+            YU: (at(xh, down), to_x, rest, at(ox, down)),
+            YD: (at(xh, up), to_x, rest, at(ox, up)),
+            F2: (at(ox, down), to_up, (0, h), at(ox, opp)),
+            G2: (at(ox, up), to_down, (h, m - h), at(ox, opp)),
+            YO: (at(xh, opp), to_x, rest, at(ox, opp)),
+        }
+
+    def copy(cls, e, p, kv, ln, target, span):
+        ref = piece(kv, ln, c, p).at[pl.ds(*span)]
         return remote(ref, ref, cs.at[cls, e], cr.at[cls, e], target)
 
     def sib(e, p, kv, ln, half):
         ref = piece(kv, ln, half, p)
         return remote(ref, ref, bs.at[e, ln], br.at[e, ln], to_sib)
 
-    shared = {
-        U1: (at(xh, y), to_up, None, at(xh, down)), D1: (at(xh, y), to_down, None, at(xh, up)),
-        X0: (at(xh, y), to_x, None, at(ox, y)),
-        FU: (at(xh, down), to_up, 0, at(xh, opp)), FD: (at(xh, up), to_down, 1, at(xh, opp)),
-    }
-    x_first = dict(shared)
-    x_first.update({
-        U2: (at(ox, y), to_up, None, at(ox, down)), D2: (at(ox, y), to_down, None, at(ox, up)),
-        F2: (at(ox, down), to_up, 0, at(ox, opp)), G2: (at(ox, up), to_down, 1, at(ox, opp)),
-    })
-    y_first = dict(shared)
-    y_first.update({
-        U2: (at(xh, down), to_x, None, at(ox, down)), D2: (at(xh, up), to_x, None, at(ox, up)),
-        F2: (at(xh, opp), to_x, None, at(ox, opp)),
-    })
-
-    def is_x_first(kv, k):
-        even = k % 2 == 0
-        return even if kv == 0 else jnp.logical_or(even, k == NZ - 1)
-
-    def modes(kv, k, body):
-        first = is_x_first(kv, k)
-
-        @pl.when(first)
-        def _():
-            body(x_first, True)
-
-        @pl.when(jnp.logical_not(first))
-        def _():
-            body(y_first, False)
-
-    def stages(kv, k, p, classes, xf, stage):
+    def stages(kv, k, p, stage):
         e = kv * NZ + k
-
-        def send(cls):
-            ln, target, rows, _ = classes[cls]
-            copy(cls, e, p, kv, ln, target, rows).start()
-
-        def wait(cls):
-            _, target, rows, ln = classes[cls]
-            copy(cls, e, p, kv, ln, target, rows).wait_recv()
-
-        def share(ln):
-            sib(e, p, kv, ln, c).start()
+        classes = routes(kv)
+
+        def send(*names):
+            for cls in names:
+                ln, target, span, _ = classes[cls]
+                copy(cls, e, p, kv, ln, target, span).start()
+
+        def wait(*names):
+            for cls in names:
+                _, target, span, ln = classes[cls]
+                copy(cls, e, p, kv, ln, target, span).wait_recv()
+
+        def share(*lines):
+            for ln in lines:
+                sib(e, p, kv, ln, c).start()
 
         if stage == 1:
             ref = piece(kv, line, c, p)
             remote(ref, ref, zs.at[kv, 0, 0], zr.at[kv, p], to_x).wait_recv()
-            for cls in (X0, U1, D1):
-                send(cls)
+            send(X0, U1, D1)
             share(line)
-        elif stage == 2 and xf:
+        elif stage == 2:
             wait(X0)
-            send(U2)
-            send(D2)
+            send(U2, D2)
             wait(U1)
-            send(FU)
+            send(YU, FU)
             wait(D1)
-            send(FD)
-            for ln in (at(ox, y), at(xh, down), at(xh, up)):
-                share(ln)
-        elif stage == 2:
-            wait(U1)
-            send(U2)
-            send(FU)
-            wait(D1)
-            send(D2)
-            send(FD)
-            for ln in (at(xh, down), at(xh, up)):
-                share(ln)
-        elif stage == 3 and xf:
+            send(YD, FD)
+            share(at(ox, y), at(xh, down), at(xh, up))
+        elif stage == 3:
             wait(U2)
             send(F2)
             wait(D2)
             send(G2)
-            wait(FU)
-            wait(FD)
-            for ln in (at(ox, down), at(ox, up), at(xh, opp)):
-                share(ln)
-        elif stage == 3:
-            wait(FU)
-            wait(FD)
-            send(F2)
-            wait(X0)
-            for ln in (at(xh, opp), at(ox, y)):
-                share(ln)
-        elif xf:
-            wait(F2)
-            wait(G2)
+            wait(FU, FD)
+            send(YO)
+            share(at(xh, opp))
+        else:
+            wait(YU, YD)
+            share(at(ox, down), at(ox, up))
+            wait(F2, G2, YO)
             share(at(ox, opp))
-        else:
-            for cls, yy in ((U2, down), (D2, up), (F2, opp)):
-                wait(cls)
-                share(at(ox, yy))
 
     def sib_received(kv):
         @pl.loop(0, NZ)
@@ -267,16 +239,21 @@
             for u in range(4):
                 fn(plane, m * 4 + u)
 
-    @pl.loop(0, ITEMS + 3)
+    @pl.loop(0, ITEMS + DELAY[4])
     def _(step):
+        for kind, lag in ((0, -Z_LEAD), (1, 5), (2, 6)):
+            @pl.when(jnp.logical_and(step >= max(lag, 0), step < NZ + lag))
+            def _():
+                z_start(step - lag, kind)
+
         for stage in (4, 3, 2, 1):
-            e = step - (stage - 1)
+            e = step - DELAY[stage]
             for kv in range(2):
                 @pl.when(jnp.logical_and(e >= kv * NZ, e < (kv + 1) * NZ))
                 def _():
                     k = e - kv * NZ
                     p = near_plane(k)
-                    modes(kv, k, lambda classes, xf: stages(kv, k, p, classes, xf, stage))
+                    stages(kv, k, p, stage)
 
         @pl.when(step == SCORES_FROM)
         def _():
@@ -355,11 +332,8 @@
         for kv in range(2):
             e = kv * NZ + k
 
-            def sent(classes, xf):
-                for cls, (ln, target, rows, _) in classes.items():
-                    copy(cls, e, p, kv, ln, target, rows).wait_send()
-
-            modes(kv, k, sent)
+            for cls, (ln, target, span, _) in routes(kv).items():
+                copy(cls, e, p, kv, ln, target, span).wait_send()
 
             @pl.loop(0, LINES)
             def _(ln):

time: 308 us -> 259 us (0.84)
  the two profiles are of different devices: /device:TPU:227 before, /device:TPU:97 now
where the time goes in v3:
time: 259 us
  Pallas kernels  245 us (95%)
  matrix products  11.1 us (4%)
    pallas_call x1, Pallas kernels, attention_call(): pl.pallas_call(attention_kernel, out_shape=jax.ShapeDtypeStruct((SHARD_BL...  245 us
    dot_general x1, matrix products, body(): jnp.dot(attended.reshape(ROWS, -1), out_weight, preferred_element_type=jn...  11.1 us

profile of v3, /device:TPU:97, one launch (start us, length us, event | category | flops | bytes accessed | tf_op | source)
XLA Modules:
  0.0 258.9 jit_solution(4367982595360726107)
XLA Ops:
  0.0 1.0 copy.6
  1.0 0.3 reshape.15
  1.3 0.1 reshape.16
  1.4 1.3 fusion.4.table
  2.8 245.0 %block_attention.1 = bf16[24,64,2048]{2,1,0:T(8,128)(2,1)} custom-call(s32[290]{0:T(512)} %fusion.4.table, bf16[24,64,512]{2,1,0:T(8,128)(2,1)} %bitcast.7, bf16[2,24,64,512]{3,2,1,0:T(8,128)(2,1)} %bitcast.6), custom_call_target="tpu_custom_call" | custom-call | tf_op jit(solution)/shard_map/block_attention/pallas_call | solution.py:347
  247.8 11.1 %convolution_convert_fusion = bf16[1536,1024]{1,0:T(8,128)(2,1)} fusion(bf16[1536,2048]{1,0:T(8,128)(2,1)} %bitcast.5, bf16[2048,1024]{1,0:T(8,128)(2,1)} %param.9), kind=kOutput, calls=%fused_computation | convolution fusion | flops 6444023808 | bytes 13631488 | tf_op jit(solution)/shard_map/dot_general | solution.py:381
  (1 shorter events, 0.0 us)

commit v4 on v3

--- a/solution.py
+++ b/solution.py
@@ -49,6 +49,10 @@
 FROM_X = (7, 6)
 Z_LEAD = 2
 ITEMS = 2 * NZ
+CHUNK = 4
+PARTS = NZ * HALF_BLOCKS // CHUNK
+LAG = 3
+WEIGHT_AT = 512
 DELAY = (0, 0, 2, 4, 6)
 SCORES_FROM = NZ + DELAY[4]
 SCALE = math.log2(math.e) / HEAD_DIM**0.5
@@ -60,7 +64,10 @@
     return ((line * NC + offset // HALF_BLOCKS) * NZ + plane) * HALF_BLOCKS + offset % HALF_BLOCKS
 
 
-def attention_kernel(table, q_ref, kv_ref, out_ref, kbuf, vbuf, qbuf, pbuf, obuf, zs, zr, cs, cr, bs, br, rzs, rzr, ras, rar):
+def attention_kernel(
+    table, q_ref, kv_ref, w_ref, out_ref, kbuf, vbuf, qbuf, pbuf, obuf,
+    zs, zr, cs, cr, bs, br, rzs, rzr, ras, rar, ws, os, ready,
+):
     xh, y, z, xl, c = coords()
     line = xh * NY + y
     up, down, opp = (y + 1) % NY, (y + NY - 1) % NY, (y + 2) % NY
@@ -233,6 +240,24 @@
         mixed = jnp.dot(pbuf[n], listed(vbuf, n, block), preferred_element_type=jnp.float32)
         obuf[n] = mixed.astype(jnp.bfloat16)
 
+    def weight_copy(g):
+        cols = pl.ds(pl.multiple_of(g * HEAD_DIM, HEAD_DIM), HEAD_DIM)
+        return pltpu.make_async_copy(w_ref.at[:, :, cols], kbuf.at[pl.ds(WEIGHT_AT + g * 32, 32)], ws.at[g])
+
+    writers = [device(xh, y, (z + dz) % NZ, xl, c) for dz in range(1, NZ)] + [to_lo, to_sib]
+
+    def sends_done(kv):
+        @pl.loop(0, NZ)
+        def _(k):
+            p = near_plane(k)
+            e = kv * NZ + k
+            for cls, (ln, target, span, _) in routes(kv).items():
+                copy(cls, e, p, kv, ln, target, span).wait_send()
+
+            @pl.loop(0, LINES)
+            def _(ln):
+                sib(e, p, kv, ln, c).wait_send()
+
     def blocks_of(plane, fn):
         @pl.loop(0, HALF_BLOCKS // 4)
         def _(m):
@@ -264,90 +289,156 @@
                 ref = qbuf.at[pl.ds(p * HALF_BLOCKS, HALF_BLOCKS)]
                 remote(ref, ref, zs.at[2, 0, 0], zr.at[2, p], to_x).wait_recv()
 
-        @pl.when(step >= SCORES_FROM)
-        def _():
-            blocks_of(step - SCORES_FROM, weigh)
+        @pl.when(jnp.logical_and(step >= SCORES_FROM, step < SCORES_FROM + NZ // 2))
+        def _():
+            for u in range(2):
+                blocks_of(2 * (step - SCORES_FROM) + u, weigh)
+
+        @pl.when(step == SCORES_FROM + NZ // 2)
+        def _():
+            sends_done(0)
+
+            @pl.loop(0, NZ)
+            def _(g):
+                weight_copy(g).start()
+
+            for writer in writers:
+                pl.semaphore_signal(ready, inc=1, device_id=writer, device_id_type=MESH)
 
     sib_received(1)
 
-    def place(half, side, plane):
-        cols = pl.ds(pl.multiple_of((side * NZ + plane) * HEAD_DIM, HEAD_DIM), HEAD_DIM)
-        return out_ref.at[pl.ds(half * HALF_BLOCKS, HALF_BLOCKS), :, cols]
-
-    def rows_of(p):
-        return obuf.at[pl.ds(p * HALF_BLOCKS, HALF_BLOCKS)]
-
-    def home(k, p):
-        return remote(rows_of(p), place(c, xl, z), rzs.at[k], rzr.at[z], device(xh, y, p, xl, c))
-
-    def onward(cls, k, half, side, p, target):
-        ref = place(half, side, p)
-        return remote(ref, ref, ras.at[cls, k], rar.at[cls, k], target)
-
-    @pl.loop(0, NZ + 4)
+    def place(half, side, plane, r):
+        return kbuf.at[pl.ds((side * NZ + plane) * SHARD_BLOCKS + half * HALF_BLOCKS + r * CHUNK, CHUNK)]
+
+    def rows_of(p, r):
+        return obuf.at[pl.ds(p * HALF_BLOCKS + r * CHUNK, CHUNK)]
+
+    def home(r, k, p):
+        return remote(rows_of(p, r), place(c, xl, z, r), rzs.at[r, k], rzr.at[r, z], device(xh, y, p, xl, c))
+
+    def onward(cls, i, half, side, p, r, target):
+        ref = place(half, side, p, r)
+        return remote(ref, ref, ras.at[cls, i], rar.at[cls, i], target)
+
+    pl.semaphore_wait(ready, len(writers))
+
+    @pl.loop(0, PARTS)
+    def _(i):
+        r, k = i // NZ, i % NZ
+        p = near_plane(k)
+        for u in range(CHUNK):
+            mix(p, r * CHUNK + u)
+
+        @pl.when(k == 0)
+        def _():
+            pltpu.make_async_copy(rows_of(z, r), place(c, xl, z, r), rzr.at[r, z]).start()
+
+        @pl.when(k > 0)
+        def _():
+            home(r, k, p).start()
+
+    def project(r, half, side):
+        for w in range(2):
+            total = jnp.zeros((CHUNK * BLOCK, 256), jnp.float32)
+            for pair in range(NZ):
+                left = [
+                    kbuf[pl.ds((2 * pair + i) * SHARD_BLOCKS + half * HALF_BLOCKS + r * CHUNK, CHUNK)]
+                    for i in range(2)
+                ]
+                right = [kbuf[pl.ds(WEIGHT_AT + ((side * 2 + w) * 2 + i) * 32 + pair * 4, 4)] for i in range(2)]
+                total = total + jnp.dot(
+                    jnp.concatenate([v.reshape(CHUNK * BLOCK, HEAD_DIM) for v in left], axis=1),
+                    jnp.concatenate([v.reshape(256, HEAD_DIM) for v in right], axis=1),
+                    preferred_element_type=jnp.float32,
+                )
+            result = total.astype(jnp.bfloat16)
+            for u in range(CHUNK):
+                pbuf[tile(r, half, side) + u, :, w * 256:(w + 1) * 256] = result[u * BLOCK:(u + 1) * BLOCK]
+
+    def tile(r, half, side):
+        return ((r * NC + half) * 2 + side) * CHUNK
+
+    def result_copy(r, half, side):
+        cols = pl.ds(pl.multiple_of(side * 512, 512), 512)
+        return pltpu.make_async_copy(
+            pbuf.at[pl.ds(tile(r, half, side), CHUNK)],
+            out_ref.at[pl.ds(half * HALF_BLOCKS + r * CHUNK, CHUNK), :, cols],
+            os.at[r, half * 2 + side],
+        )
+
+    @pl.loop(0, PARTS + LAG + NZ)
     def _(step):
-        @pl.when(step < NZ)
-        def _():
-            p = near_plane(step)
-            blocks_of(p, mix)
-
-            @pl.when(step == 0)
+        @pl.when(step < PARTS)
+        def _():
+            r, k = step // NZ, step % NZ
+            p = near_plane(k)
+            ref = place(c, xl, p, r)
+            remote(ref, ref, rzs.at[0, 0], rzr.at[r, p], to_lo).wait_recv()
+            onward(0, step, c, xl, p, r, to_lo).start()
+            onward(1, step, c, xl, p, r, to_sib).start()
+
+        @pl.when(jnp.logical_and(step >= 2, step < PARTS + 2))
+        def _():
+            i = step - 2
+            r, p = i // NZ, near_plane(i % NZ)
+            onward(0, i, c, 1 - xl, p, r, to_lo).wait_recv()
+            onward(2, i, c, 1 - xl, p, r, to_sib).start()
+
+        done = step - LAG - NZ
+
+        @pl.when(jnp.logical_and(done >= 0, done % NZ == 0))
+        def _():
+            @pl.when(done == 0)
             def _():
-                pltpu.make_async_copy(rows_of(z), place(c, xl, z), rzr.at[z]).start()
-
-            @pl.when(step > 0)
-            def _():
-                home(step, p).start()
-
-        @pl.when(jnp.logical_and(step >= 2, step < NZ + 2))
-        def _():
-            k = step - 2
-            p = near_plane(k)
-            remote(place(c, xl, p), place(c, xl, p), rzs.at[0], rzr.at[p], to_lo).wait_recv()
-            onward(0, k, c, xl, p, to_lo).start()
-            onward(1, k, c, xl, p, to_sib).start()
-
-        @pl.when(step >= 4)
-        def _():
-            k = step - 4
-            p = near_plane(k)
-            onward(0, k, c, 1 - xl, p, to_lo).wait_recv()
-            onward(2, k, c, 1 - xl, p, to_sib).start()
+                @pl.loop(0, NZ)
+                def _(g):
+                    weight_copy(g).wait()
+
+            @pl.loop(0, NZ)
+            def _(k):
+                p = near_plane(k)
+                onward(1, done + k, 1 - c, xl, p, done // NZ, to_sib).wait_recv()
+                onward(2, done + k, 1 - c, 1 - xl, p, done // NZ, to_sib).wait_recv()
+
+        @pl.when(jnp.logical_and(done >= 0, done % 2 == 0))
+        def _():
+            r, part = done // NZ, (done % NZ) // 2
+            project(r, part // 2, part % 2)
+            result_copy(r, part // 2, part % 2).start()
+
+    @pl.loop(0, PARTS)
+    def _(i):
+        r, k = i // NZ, i % NZ
+        p = near_plane(k)
+
+        @pl.when(k > 0)
+        def _():
+            home(r, k, p).wait_send()
+
+        onward(0, i, c, xl, p, r, to_lo).wait_send()
+        onward(1, i, c, xl, p, r, to_sib).wait_send()
+        onward(2, i, c, 1 - xl, p, r, to_sib).wait_send()
+
+    sends_done(1)
 
     @pl.loop(0, NZ)
     def _(k):
-        p = near_plane(k)
-
-        @pl.when(k > 0)
-        def _():
-            home(k, p).wait_send()
-
-        onward(0, k, c, xl, p, to_lo).wait_send()
-        onward(1, k, c, xl, p, to_sib).wait_send()
-        onward(2, k, c, 1 - xl, p, to_sib).wait_send()
-        onward(1, k, 1 - c, xl, p, to_sib).wait_recv()
-        onward(2, k, 1 - c, 1 - xl, p, to_sib).wait_recv()
         for kind in range(3):
             z_each(k, kind, lambda d: d.wait_send(), None)
-        for kv in range(2):
-            e = kv * NZ + k
-
-            for cls, (ln, target, span, _) in routes(kv).items():
-                copy(cls, e, p, kv, ln, target, span).wait_send()
-
-            @pl.loop(0, LINES)
-            def _(ln):
-                sib(e, p, kv, ln, c).wait_send()
-
-
-def attention_call(table, queries, keys_values):
+
+    for r in range(HALF_BLOCKS // CHUNK):
+        for part in range(4):
+            result_copy(r, part // 2, part % 2).wait()
+
+
+def attention_call(table, queries, keys_values, weight):
     anyspace = pl.BlockSpec(memory_space=pl.ANY)
     dma = pltpu.SemaphoreType.DMA
     key_blocks = LINES * LINE_BLOCKS
     return pl.pallas_call(
         attention_kernel,
-        out_shape=jax.ShapeDtypeStruct((SHARD_BLOCKS, BLOCK, NXL * NZ * HEAD_DIM), jnp.bfloat16),
-        in_specs=[pl.BlockSpec(memory_space=pltpu.SMEM), anyspace, anyspace],
+        out_shape=jax.ShapeDtypeStruct((SHARD_BLOCKS, BLOCK, weight.shape[-1]), jnp.bfloat16),
+        in_specs=[pl.BlockSpec(memory_space=pltpu.SMEM), anyspace, anyspace, anyspace],
         out_specs=anyspace,
         scratch_shapes=[
             pltpu.VMEM((key_blocks, BLOCK, HEAD_DIM), jnp.bfloat16),
@@ -358,13 +449,14 @@
             dma((3, NC, NZ)), dma((3, NZ)),
             dma((NCLASS, ITEMS)), dma((NCLASS, ITEMS)),
             dma((ITEMS, LINES)), dma((ITEMS, LINES)),
-            dma((NZ,)), dma((NZ,)), dma((3, NZ)), dma((3, NZ)),
+            dma((HALF_BLOCKS // CHUNK, NZ)), dma((HALF_BLOCKS // CHUNK, NZ)), dma((3, PARTS)), dma((3, PARTS)),
+            dma((NZ,)), dma((HALF_BLOCKS // CHUNK, 4)), pltpu.SemaphoreType.REGULAR,
         ],
         compiler_params=pltpu.CompilerParams(
             collective_id=1, has_side_effects=True, vmem_limit_bytes=60 * 1024 * 1024
         ),
         name="block_attention",
-    )(table, queries, keys_values)
+    )(table, queries, keys_values, weight)
 
 
 def body(queries, keys_values, global_ids, rand_ids, out_weight):
@@ -373,13 +465,13 @@
     lists = rand_ids.reshape(LINES, NZ, NC, HALF_BLOCKS * NRANDOM)
     mine = lax.dynamic_slice(lists, (xh * NY + y, 0, c, 0), (1, NZ, 1, HALF_BLOCKS * NRANDOM)).reshape(-1)
     table = address(jnp.concatenate([mine, global_ids]))
-    attended = attention_call(
+    projected = attention_call(
         table,
         queries.reshape(SHARD_BLOCKS, BLOCK, width),
         keys_values.reshape(2, SHARD_BLOCKS, BLOCK, width),
+        out_weight.reshape(-1, BLOCK, out_weight.shape[1]),
     )
-    summed = jnp.dot(attended.reshape(ROWS, -1), out_weight, preferred_element_type=jnp.float32)
-    return summed.astype(jnp.bfloat16)
+    return projected.reshape(ROWS, -1)
 
 
 def solution(mesh):

time: 259 us -> 244 us (0.942); the launches traced: 259 us -> 241 us
  matrix products: 11.1 us -> 0 us
  Pallas kernels: 245 us -> 234 us
  local copies, waits for them, and re-layouts: 1.4 us -> 5.26 us
    dot_general x1 -> x0, matrix products: 11.1 us -> none  [body(): jnp.dot(attended.reshape(ROWS, -1), out_weight, preferred_element_type=jn...]
    pallas_call x1, Pallas kernels: 245 us -> 234 us  [attention_call(): pl.pallas_call(attention_kernel, out_shape=jax.ShapeDtypeStruct((SHARD_BL...]
    unnamed x1 -> x2, local copies, waits for them, and re-layouts: 1.02 us -> 4.88 us
where the time goes in v4:
time: 244 us; the launch traced here: 241 us
  Pallas kernels  234 us (96%)
  local copies, waits for them, and re-layouts  5.26 us (2%)
    pallas_call x1, Pallas kernels, attention_call(): pl.pallas_call(attention_kernel, out_shape=jax.ShapeDtypeStruct((SHARD_BL...  234 us
    unnamed x2, local copies, waits for them, and re-layouts  4.88 us

profile of v4, /device:TPU:97, one launch (start us, length us, event | category | flops | bytes accessed | tf_op | source)
XLA Modules:
  0.0 240.8 jit_solution(7802453854325061095)
XLA Ops:
  0.0 1.0 copy.6
  1.0 0.3 reshape.18
  1.3 0.1 reshape.19
  1.4 1.3 fusion.4.table
  2.8 234.2 %block_attention.1 = bf16[24,64,1024]{2,1,0:T(8,128)(2,1)} custom-call(s32[290]{0:T(512)} %fusion.4.table, bf16[24,64,512]{2,1,0:T(8,128)(2,1)} %bitcast.7, bf16[2,24,64,512]{3,2,1,0:T(8,128)(2,1)} %bitcast.6, bf16[32,64,1024]{2,1,0:T(8,128)(2,1)} %bitcast.5), custom_call_target="tpu_custom_call" | custom-call | tf_op jit(solution)/shard_map/block_attention/pallas_call | solution.py:438
  236.9 3.9 %copy.8 = bf16[1536,1024]{1,0:T(8,128)(2,1)} copy(bf16[1536,1024]{1,0:T(8,128)(2,1)} %bitcast.4) | data formatting | bytes 6291456
  (1 shorter events, 0.0 us)

commit v5 on v4

--- a/solution.py
+++ b/solution.py
@@ -51,6 +51,7 @@
 ITEMS = 2 * NZ
 CHUNK = 4
 PARTS = NZ * HALF_BLOCKS // CHUNK
+FORWARD = 6
 LAG = 3
 WEIGHT_AT = 512
 DELAY = (0, 0, 2, 4, 6)
@@ -322,21 +323,6 @@
 
     pl.semaphore_wait(ready, len(writers))
 
-    @pl.loop(0, PARTS)
-    def _(i):
-        r, k = i // NZ, i % NZ
-        p = near_plane(k)
-        for u in range(CHUNK):
-            mix(p, r * CHUNK + u)
-
-        @pl.when(k == 0)
-        def _():
-            pltpu.make_async_copy(rows_of(z, r), place(c, xl, z, r), rzr.at[r, z]).start()
-
-        @pl.when(k > 0)
-        def _():
-            home(r, k, p).start()
-
     def project(r, half, side):
         for w in range(2):
             total = jnp.zeros((CHUNK * BLOCK, 256), jnp.float32)
@@ -356,7 +342,7 @@
                 pbuf[tile(r, half, side) + u, :, w * 256:(w + 1) * 256] = result[u * BLOCK:(u + 1) * BLOCK]
 
     def tile(r, half, side):
-        return ((r * NC + half) * 2 + side) * CHUNK
+        return (half * 2 + side) * HALF_BLOCKS + r * CHUNK
 
     def result_copy(r, half, side):
         cols = pl.ds(pl.multiple_of(side * 512, 512), 512)
@@ -366,9 +352,26 @@
             os.at[r, half * 2 + side],
         )
 
-    @pl.loop(0, PARTS + LAG + NZ)
-    def _(step):
-        @pl.when(step < PARTS)
+    @pl.loop(0, PARTS + FORWARD + LAG + NZ)
+    def _(tick):
+        @pl.when(tick < PARTS)
+        def _():
+            r, k = tick // NZ, tick % NZ
+            p = near_plane(k)
+            for u in range(CHUNK):
+                mix(p, r * CHUNK + u)
+
+            @pl.when(k == 0)
+            def _():
+                pltpu.make_async_copy(rows_of(z, r), place(c, xl, z, r), rzr.at[r, z]).start()
+
+            @pl.when(k > 0)
+            def _():
+                home(r, k, p).start()
+
+        step = tick - FORWARD
+
+        @pl.when(jnp.logical_and(step >= 0, step < PARTS))
         def _():
             r, k = step // NZ, step % NZ
             p = near_plane(k)

time: 244 us -> 241 us (0.988)
  no operation moved by 1% of the time
where the time goes in v5:
time: 241 us; the launch traced here: 238 us
  Pallas kernels  232 us (96%)
  local copies, waits for them, and re-layouts  5.26 us (2%)
    pallas_call x1, Pallas kernels, attention_call(): pl.pallas_call(attention_kernel, out_shape=jax.ShapeDtypeStruct((SHARD_BL...  232 us
    unnamed x2, local copies, waits for them, and re-layouts  4.88 us

profile of v5, /device:TPU:97, one launch (start us, length us, event | category | flops | bytes accessed | tf_op | source)
XLA Modules:
  0.0 238.4 jit_solution(8754997738473901662)
XLA Ops:
  0.0 1.0 copy.6
  1.0 0.3 reshape.18
  1.3 0.1 reshape.19
  1.4 1.3 fusion.4.table
  2.8 231.8 %block_attention.1 = bf16[24,64,1024]{2,1,0:T(8,128)(2,1)} custom-call(s32[290]{0:T(512)} %fusion.4.table, bf16[24,64,512]{2,1,0:T(8,128)(2,1)} %bitcast.7, bf16[2,24,64,512]{3,2,1,0:T(8,128)(2,1)} %bitcast.6, bf16[32,64,1024]{2,1,0:T(8,128)(2,1)} %bitcast.5), custom_call_target="tpu_custom_call" | custom-call | tf_op jit(solution)/shard_map/block_attention/pallas_call | solution.py:441
  234.6 3.9 %copy.8 = bf16[1536,1024]{1,0:T(8,128)(2,1)} copy(bf16[1536,1024]{1,0:T(8,128)(2,1)} %bitcast.4) | data formatting | bytes 6291456
  (1 shorter events, 0.0 us)

commit v6 on v5

--- a/solution.py
+++ b/solution.py
@@ -52,7 +52,8 @@
 CHUNK = 4
 PARTS = NZ * HALF_BLOCKS // CHUNK
 FORWARD = 6
-LAG = 3
+RELAY = 5
+LAG = 6
 WEIGHT_AT = 512
 DELAY = (0, 0, 2, 4, 6)
 SCORES_FROM = NZ + DELAY[4]
@@ -380,9 +381,9 @@
             onward(0, step, c, xl, p, r, to_lo).start()
             onward(1, step, c, xl, p, r, to_sib).start()
 
-        @pl.when(jnp.logical_and(step >= 2, step < PARTS + 2))
-        def _():
-            i = step - 2
+        @pl.when(jnp.logical_and(step >= RELAY, step < PARTS + RELAY))
+        def _():
+            i = step - RELAY
             r, p = i // NZ, near_plane(i % NZ)
             onward(0, i, c, 1 - xl, p, r, to_lo).wait_recv()
             onward(2, i, c, 1 - xl, p, r, to_sib).start()

time: 241 us -> 238 us (0.988)
  Pallas kernels: 232 us -> 229 us
    pallas_call x1, Pallas kernels: 232 us -> 229 us  [attention_call(): pl.pallas_call(attention_kernel, out_shape=jax.ShapeDtypeStruct((SHARD_BL...]
where the time goes in v6:
time: 238 us; the launch traced here: 236 us
  Pallas kernels  229 us (96%)
  local copies, waits for them, and re-layouts  5.26 us (2%)
    pallas_call x1, Pallas kernels, attention_call(): pl.pallas_call(attention_kernel, out_shape=jax.ShapeDtypeStruct((SHARD_BL...  229 us
    unnamed x2, local copies, waits for them, and re-layouts  4.88 us

profile of v6, /device:TPU:97, one launch (start us, length us, event | category | flops | bytes accessed | tf_op | source)
XLA Modules:
  0.0 235.6 jit_solution(11344064124813730491)
XLA Ops:
  0.0 1.0 copy.6
  1.0 0.3 reshape.18
  1.3 0.1 reshape.19
  1.4 1.3 fusion.4.table
  2.8 228.9 %block_attention.1 = bf16[24,64,1024]{2,1,0:T(8,128)(2,1)} custom-call(s32[290]{0:T(512)} %fusion.4.table, bf16[24,64,512]{2,1,0:T(8,128)(2,1)} %bitcast.7, bf16[2,24,64,512]{3,2,1,0:T(8,128)(2,1)} %bitcast.6, bf16[32,64,1024]{2,1,0:T(8,128)(2,1)} %bitcast.5), custom_call_target="tpu_custom_call" | custom-call | tf_op jit(solution)/shard_map/block_attention/pallas_call | solution.py:442
  231.7 3.9 %copy.8 = bf16[1536,1024]{1,0:T(8,128)(2,1)} copy(bf16[1536,1024]{1,0:T(8,128)(2,1)} %bitcast.4) | data formatting | bytes 6291456
  (1 shorter events, 0.0 us)

commit v7 on v6

--- a/solution.py
+++ b/solution.py
@@ -49,11 +49,11 @@
 FROM_X = (7, 6)
 Z_LEAD = 2
 ITEMS = 2 * NZ
-CHUNK = 4
+CHUNK = 3
 PARTS = NZ * HALF_BLOCKS // CHUNK
-FORWARD = 6
-RELAY = 5
-LAG = 6
+FORWARD = 8
+RELAY = 8
+LAG = 9
 WEIGHT_AT = 512
 DELAY = (0, 0, 2, 4, 6)
 SCORES_FROM = NZ + DELAY[4]

time: 238 us -> 238 us (level)
  no operation moved by 1% of the time
where the time goes in v7:
time: 238 us; the launch traced here: 236 us
  Pallas kernels  230 us (97%)
  local copies, waits for them, and re-layouts  5.26 us (2%)
    pallas_call x1, Pallas kernels, attention_call(): pl.pallas_call(attention_kernel, out_shape=jax.ShapeDtypeStruct((SHARD_BL...  230 us
    unnamed x2, local copies, waits for them, and re-layouts  4.88 us

profile of v7, /device:TPU:97, one launch (start us, length us, event | category | flops | bytes accessed | tf_op | source)
XLA Modules:
  0.0 236.3 jit_solution(3282497583175066047)
XLA Ops:
  0.0 1.0 copy.6
  1.0 0.3 reshape.18
  1.3 0.1 reshape.19
  1.4 1.3 fusion.4.table
  2.8 229.7 %block_attention.1 = bf16[24,64,1024]{2,1,0:T(8,128)(2,1)} custom-call(s32[290]{0:T(512)} %fusion.4.table, bf16[24,64,512]{2,1,0:T(8,128)(2,1)} %bitcast.7, bf16[2,24,64,512]{3,2,1,0:T(8,128)(2,1)} %bitcast.6, bf16[32,64,1024]{2,1,0:T(8,128)(2,1)} %bitcast.5), custom_call_target="tpu_custom_call" | custom-call | tf_op jit(solution)/shard_map/block_attention/pallas_call | solution.py:442
  232.5 3.9 %copy.8 = bf16[1536,1024]{1,0:T(8,128)(2,1)} copy(bf16[1536,1024]{1,0:T(8,128)(2,1)} %bitcast.4) | data formatting | bytes 6291456
  (1 shorter events, 0.0 us)
